TPU v7x, 32 devices: a whole 2x2x4 slice. The times are simulated.
32 devices in a mesh: kv: 2 (over x), seq: 16 (over z, y, core).
Axes of the slice: x: 2, y: 2, z: 4, core: 2. Of those that a mesh axis runs over, the one named last changes fastest.
Arguments:
- hidden: bfloat16 [1024, 2048], P('seq', 'kv'), may hold values from -1.5 to 1.5
- in_gain: float32 [2048], replicated, may hold values from 0.5 to 1.5
- w_query: bfloat16 [2048, 2048], P(None, 'kv'), may hold values from -0.125 to 0.125
- key_projection_weight: bfloat16 [2048, 1024], P(None, 'kv'), may hold values from -0.125 to 0.125
- value_projection_weight: bfloat16 [2048, 1024], P(None, 'kv'), may hold values from -0.125 to 0.125
- w_gate: bfloat16 [2048, 16], P(None, 'kv'), may hold values from -0.125 to 0.125
- w_out: bfloat16 [2048, 2048], P('kv'), may hold values from -0.125 to 0.125
- q_gain: float32 [128], replicated, may hold values from 0.1 to 1.9
- k_gain: float32 [128], replicated, may hold values from 0.1 to 1.9
- cache_keys: bfloat16 [32768, 8, 128], P('seq', 'kv'), may hold values from -160 to 160
- pooled_cache_values: bfloat16 [32768, 8, 128], P('seq', 'kv'), may hold values from -6 to 6
- prefix_len: int32 [4], replicated, may hold values from 1024 to 8192, as said below
- own_len: int32 [32], replicated, may hold values from 256 to 2048, as said below
- request_group: int32 [32], replicated, may hold values from 0 to 3, as said below
- parents: int32 [32, 32], P('seq'), may hold values from 0 to 30, as said below
- accepted_leaf: int32 [32], P('seq'), may hold values from 0 to 31
Outputs:
- layer_out: bfloat16 [1024, 2048], P('seq', 'kv')
- accepted_keys: bfloat16 [32, 32, 1024], P('seq', None, 'kv')
- accepted_values: bfloat16 [32, 32, 1024], P('seq', None, 'kv')
Inputs may be any that keep to these rules, and one draw needn't show every extreme that they name: parents[r, 0] is 0 and node 0 is the root; for i >= 1, parents[r, i] < i. `prefix_len`: the lengths sum to 32768 // 2; one is exactly 8192 and one exactly 1024. `own_len`: the lengths sum to 32768 // 2; one is exactly 2048 and one exactly 256. `request_group`: every group holds exactly 8 requests.
All inputs are finite; a program needn't handle non-finite values.
Results may differ from a plain program's by a relative error of at most 0.017.
The roundings to bfloat16 on the way count: a program that leaves them out, or rounds other values in their place, can miss the bound.
Values may be sent and summed in bfloat16 or wider, within the bound.
A program may use at most 128 MiB of HBM per device.

v0:
```python
import math
import jax
import jax.numpy as jnp
from jax import lax
from jax.sharding import PartitionSpec as P

EPSILON = 1e-06
ROPE_BASE = 1000000.0
NEGATIVE = -1e30


def rms_scale(values, scales):
    mean_square = jnp.mean(values * values, axis=-1, keepdims=True)
    return values * lax.rsqrt(mean_square + EPSILON) * scales


def rotate_pairs(values, positions):
    half_width = values.shape[-1] // 2
    freqs = jnp.exp(
        jnp.arange(half_width, dtype=jnp.float32) * (-2.0 * math.log(ROPE_BASE) / values.shape[-1])
    )
    angles = positions[:, None] * freqs[None, :]
    cosine = jnp.concatenate([jnp.cos(angles), jnp.cos(angles)], axis=-1)[:, None, :]
    sine = jnp.concatenate([jnp.sin(angles), jnp.sin(angles)], axis=-1)[:, None, :]
    turned = jnp.concatenate([-values[..., half_width:], values[..., :half_width]], axis=-1)
    return values * cosine + turned * sine


def tree_paths(parents):
    width = parents.shape[-1]
    nodes = jnp.arange(width, dtype=jnp.int32)
    linked = (parents[:, :, None] == nodes[None, None, :]).astype(jnp.float32)
    identity_mat = jnp.eye(width, dtype=jnp.float32)
    reach = jnp.minimum(identity_mat[None] + linked * (1.0 - identity_mat[None]), 1.0)
    for squaring in range(max(1, (width - 1).bit_length())):
        reach = jnp.minimum(
            jnp.einsum("mij,mjk->mik", reach, reach, precision=lax.Precision.HIGHEST), 1.0
        )
    depth_f = jnp.sum(reach, axis=-1) - 1.0
    return (reach, depth_f)


def accepted_rows(reach, depth_f, leaves, tree_rows):
    width = reach.shape[-1]
    nodes = jnp.arange(width, dtype=jnp.int32)
    leaf_pick = (leaves[:, None] == nodes[None, :]).astype(jnp.float32)
    on_path = jnp.einsum("mi,mij->mj", leaf_pick, reach, precision=lax.Precision.HIGHEST)
    levels = (depth_f[:, None, :] == nodes.astype(jnp.float32)[None, :, None]).astype(jnp.float32)
    select = levels * on_path[:, None, :]
    return jnp.einsum(
        "mdj,mjc->mdc", select, tree_rows.astype(jnp.float32), precision=lax.Precision.HIGHEST
    ).astype(jnp.bfloat16)


def body(
    hidden,
    in_gain,
    w_query,
    key_projection_weight,
    value_projection_weight,
    w_gate,
    w_out,
    q_gain,
    k_gain,
    cache_keys,
    pooled_cache_values,
    prefix_len,
    own_len,
    request_group,
    parents,
    accepted_leaf,
):
    local_req, tree = parents.shape
    groups = prefix_len.shape[0]
    requests = own_len.shape[0]
    head_width = q_gain.shape[0]
    local_heads = w_gate.shape[1]
    local_kv = key_projection_weight.shape[1] // head_width
    per_kv = local_heads // local_kv
    local_tok = hidden.shape[0]
    pool_dev = cache_keys.shape[0]
    seq_index = lax.axis_index("seq")
    score_scale = 1.0 / math.sqrt(head_width)
    full_rows = lax.all_gather(hidden, "kv", axis=1, tiled=True)
    normed = rms_scale(full_rows.astype(jnp.float32), in_gain).astype(jnp.bfloat16)
    reach, depth_f = tree_paths(parents)
    all_reqs = jnp.arange(requests, dtype=jnp.int32)
    my_reqs = seq_index * local_req + jnp.arange(local_req, dtype=jnp.int32)
    my_pick = (my_reqs[:, None] == all_reqs[None, :]).astype(jnp.int32)
    my_group = jnp.sum(my_pick * request_group[None, :], axis=1)
    group_ids = jnp.arange(groups, dtype=jnp.int32)
    group_pick = (my_group[:, None] == group_ids[None, :]).astype(jnp.int32)
    context = jnp.sum(group_pick * prefix_len[None, :], axis=1) + jnp.sum(
        my_pick * own_len[None, :], axis=1
    )
    positions = (context[:, None].astype(jnp.float32) + depth_f).reshape(-1)
    query = jnp.dot(normed, w_query, preferred_element_type=jnp.float32).reshape(
        local_tok, local_heads, head_width
    )
    query = rotate_pairs(rms_scale(query, q_gain), positions).astype(jnp.bfloat16)
    key_new = jnp.dot(normed, key_projection_weight, preferred_element_type=jnp.float32).reshape(
        local_tok, local_kv, head_width
    )
    key_new = rotate_pairs(rms_scale(key_new, k_gain), positions).astype(jnp.bfloat16)
    value_new = (
        jnp.dot(normed, value_projection_weight, preferred_element_type=jnp.float32)
        .astype(jnp.bfloat16)
        .reshape(local_tok, local_kv, head_width)
    )
    gate_logit = jnp.dot(normed, w_gate, preferred_element_type=jnp.float32)
    tree_query = query.reshape(local_req, tree, local_kv, per_kv, head_width)
    tree_keys = key_new.reshape(local_req, tree, local_kv, head_width)
    tree_values = value_new.reshape(local_req, tree, local_kv, head_width)
    tree_scores = (
        jnp.einsum("atkgd,askd->atkgs", tree_query, tree_keys, preferred_element_type=jnp.float32)
        * score_scale
    )
    tree_seen = (reach > 0.5)[:, :, None, None, :]
    tree_scores = jnp.where(tree_seen, tree_scores, NEGATIVE)
    tree_max = jnp.max(tree_scores, axis=-1)
    tree_weights = jnp.where(tree_seen, jnp.exp(tree_scores - tree_max[..., None]), 0.0)
    tree_sum = jnp.sum(tree_weights, axis=-1).reshape(local_tok, local_heads)
    tree_num = jnp.einsum(
        "atkgs,askd->atkgd",
        tree_weights.astype(jnp.bfloat16),
        tree_values,
        preferred_element_type=jnp.float32,
    ).reshape(local_tok, local_heads, head_width)
    tree_max = tree_max.reshape(local_tok, local_heads)
    lengths_all = jnp.concatenate([prefix_len, own_len])
    starts = jnp.cumsum(lengths_all) - lengths_all
    slot_ids = seq_index * pool_dev + jnp.arange(pool_dev, dtype=jnp.int32)
    slot_segment = jnp.sum((starts[None, :] <= slot_ids[:, None]).astype(jnp.int32), axis=1) - 1
    block_len = min(512, pool_dev)
    block_count = pool_dev // block_len
    key_blocks = cache_keys.reshape(block_count, block_len, local_kv, head_width)
    value_blocks = pooled_cache_values.reshape(block_count, block_len, local_kv, head_width)
    segment_blocks = slot_segment.reshape(block_count, block_len)
    query_flat = query.reshape(local_tok, local_heads * head_width)
    query_piece = lax.all_gather(query_flat, "seq", axis=0, tiled=True)
    row_ids = jnp.arange(query_piece.shape[0], dtype=jnp.int32)
    owners = row_ids // tree
    count = query_piece.shape[0]
    grouped = query_piece.reshape(count, local_kv, per_kv, head_width)
    owner_pick = (owners[:, None] == all_reqs[None, :]).astype(jnp.int32)
    known = owners >= 0
    prefix_segment = jnp.where(known, jnp.sum(owner_pick * request_group[None, :], axis=1), -5)
    own_segment = jnp.where(known, owners + groups, -5)

    def visit(carry, block):
        run_max, run_sum, run_num = carry
        keys_block, values_block, segment_block = block
        scores = (
            jnp.einsum("nkgd,pkd->nkgp", grouped, keys_block, preferred_element_type=jnp.float32)
            * score_scale
        )
        visible = (segment_block[None, :] == prefix_segment[:, None]) | (
            segment_block[None, :] == own_segment[:, None]
        )
        visible = visible[:, None, None, :]
        scores = jnp.where(visible, scores, NEGATIVE)
        new_max = jnp.maximum(run_max, jnp.max(scores, axis=-1))
        weights = jnp.where(visible, jnp.exp(scores - new_max[..., None]), 0.0)
        factor = jnp.exp(run_max - new_max)
        run_sum = run_sum * factor + jnp.sum(weights, axis=-1)
        run_num = run_num * factor[..., None] + jnp.einsum(
            "nkgp,pkd->nkgd",
            weights.astype(jnp.bfloat16),
            values_block,
            preferred_element_type=jnp.float32,
        )
        return ((new_max, run_sum, run_num), None)

    start_state = (
        jnp.full((count, local_kv, per_kv), NEGATIVE, jnp.float32),
        jnp.zeros((count, local_kv, per_kv), jnp.float32),
        jnp.zeros((count, local_kv, per_kv, head_width), jnp.float32),
    )
    final_state, unused = lax.scan(visit, start_state, (key_blocks, value_blocks, segment_blocks))
    run_max, run_sum, run_num = final_state
    part_max = run_max.reshape(count, local_heads)
    part_sum = run_sum.reshape(count, local_heads)
    part_num = run_num.reshape(count, local_heads * head_width)
    all_rows = part_max.shape[0]
    cache_max = lax.pmax(part_max.astype(jnp.bfloat16), "seq").astype(part_max.dtype)
    factor = jnp.exp(part_max - cache_max)
    scaled_num = (part_num.reshape(all_rows, local_heads, head_width) * factor[..., None]).reshape(
        all_rows, local_heads * head_width
    )
    summed_num, summed_sum = (
        lax.psum_scatter(
            scaled_num.astype(jnp.bfloat16), "seq", scatter_dimension=0, tiled=True
        ).astype(jnp.float32),
        lax.psum_scatter(
            (part_sum * factor).astype(jnp.bfloat16), "seq", scatter_dimension=0, tiled=True
        ).astype(jnp.float32),
    )
    own_max = lax.dynamic_slice_in_dim(cache_max, seq_index * local_tok, local_tok, 0)
    final_max = jnp.maximum(own_max, tree_max)
    cache_factor = jnp.exp(own_max - final_max)
    tree_factor = jnp.exp(tree_max - final_max)
    weight_sum = summed_sum * cache_factor + tree_sum * tree_factor
    mixed = (
        summed_num.reshape(local_tok, local_heads, head_width) * cache_factor[..., None]
        + tree_num * tree_factor[..., None]
    )
    mixed = mixed / weight_sum[..., None]
    attended = (
        (mixed * jax.nn.sigmoid(gate_logit)[..., None])
        .astype(jnp.bfloat16)
        .reshape(local_tok, local_heads * head_width)
    )
    projected = jnp.dot(attended, w_out, preferred_element_type=jnp.float32)
    layer_part = lax.psum_scatter(
        projected.astype(jnp.bfloat16), "kv", scatter_dimension=1, tiled=True
    ).astype(jnp.float32)
    layer_out = (layer_part + hidden.astype(jnp.float32)).astype(jnp.bfloat16)
    tree_rows = jnp.concatenate(
        [
            key_new.reshape(local_req, tree, local_kv * head_width),
            value_new.reshape(local_req, tree, local_kv * head_width),
        ],
        axis=-1,
    )
    picked = accepted_rows(reach, depth_f, accepted_leaf, tree_rows)
    accepted_keys = picked[:, :, : local_kv * head_width]
    accepted_values = picked[:, :, local_kv * head_width :]
    return (layer_out, accepted_keys, accepted_values)


def solution(mesh):
    in_specs = (
        P("seq", "kv"),
        P(),
        P(None, "kv"),
        P(None, "kv"),
        P(None, "kv"),
        P(None, "kv"),
        P("kv", None),
        P(),
        P(),
        P("seq", "kv", None),
        P("seq", "kv", None),
        P(),
        P(),
        P(),
        P("seq", None),
        P("seq"),
    )
    out_specs = (P("seq", "kv"), P("seq", None, "kv"), P("seq", None, "kv"))
    return jax.shard_map(body, mesh=mesh, in_specs=in_specs, out_specs=out_specs, check_vma=False)
```

profile of v0, /device:TPU:0, one launch (start us, length us, event | category | flops | bytes accessed | tf_op | source)
XLA Modules:
  0.0 365.4 jit_solution(637547949621892404)
XLA Ops:
  7.3 0.8 broadcast_bitcast_fusion
  8.1 7.4 %all_gather.6 = bf16[64,2048]{1,0:T(8,128)(2,1)S(1)} all-gather(bf16[64,1024]{1,0:T(8,128)(2,1)} %param.18), channel_id=1, replica_groups=mesh['kv'=2,'seq'=16] {'kv'}, dimensions={1}, use_global_device_ids=true | all-gather | bytes 393216 | tf_op jit(solution)/shard_map/all_gather | solution.py:84
  15.6 3.1 fusion.96
  22.7 0.8 fusion.35
  25.8 0.9 fusion.28
  26.7 39.9 %all-gather.2.cloned.1.call-done = bf16[1024,1024]{1,0:T(8,128)(2,1)} async-done(((bf16[64,1024]{1,0:T(8,128)(2,1)}), bf16[1024,1024]{1,0:T(8,128)(2,1)}) %all-gather.2.cloned.1.call-update) | async-done | bytes 2097168 | tf_op jit(solution)/shard_map/all_gather | solution.py:140
  66.6 4.5 %reshape.343 = bf16[1024,4,2,128]{3,2,1,0:T(2,128)(2,1)} reshape(bf16[1024,1024]{1,0:T(8,128)(2,1)} %all-gather.2.cloned.1.call-done) | data formatting | bytes 4194304 | tf_op jit(solution)/shard_map/reshape | solution.py:144
  71.1 3.2 copy.172
  74.3 84.1 %while.15 = (s32[]{:T(128)}, f32[1024,4,2]{0,2,1:T(2,128)S(1)}, f32[1024,4,2]{0,2,1:T(2,128)S(1)}, f32[1024,4,2,128]{0,3,2,1:T(8,128)}, s32[4,512]{1,0:T(4,128)S...) while((s32[]{:T(128)}, f32[1024,4,2]{0,2,1:T(2,128)S(1)}, ...), condition=%wide.region_12.13_spmd.clone, body=%wide.region_9.12_spmd.clone.sunk | while | flops 2206780416 | bytes 69748896 | solution.py:179
  74.7 2.4 constant_dynamic-slice_fusion.6
  77.1 1.1 copy.285
  78.2 4.6 %fusion.137 = (f32[1024,4,2]{0,2,1:T(2,128)S(1)}, f32[4,512,1024,2]{2,1,3,0:T(8,128)S(1)}) fusion(pred[1024,512]{0,1:T(8,128)(4,1)S(1)} %compare_or_fusion.2, bf16[1024,4,2,128]{3,0,2,1:T(8,128)(2,1)} %get-tuple-element.291, bf16[1,512,4,128]{3,2,1,0:T(4,128)(2,1)} %get-tuple-element.256), kind=kOutput, calls=%fused_computation.3.clone.1 | convolution fusion | flops 1086316544 | bytes 19955712 | tf_op jit(solution)/shard_map/while/body/eval_jaxpr/nkgd,pkd->nkgp/dot_general | solution.py:154
  82.8 4.1 %fusion.139 = f32[1024,4,2]{0,2,1:T(2,128)S(1)} fusion(f32[4,512,1024,2]{2,1,3,0:T(8,128)S(1)} %get-tuple-element.258, f32[1024,4,2]{0,2,1:T(2,128)S(1)} %fusion.138, pred[1024,512]{0,1:T(8,128)(4,1)S(1)} %compare_or_fusion.2), kind=kLoop, calls=%fused_computation.5.clone.1 | loop fusion | flops 20963328 | bytes 17367040 | tf_op jit(solution)/shard_map/while/body/eval_jaxpr/reduce_sum | solution.py:165
  87.0 7.1 %bitcast_add_fusion.2 = f32[1024,4,2,128]{0,3,2,1:T(8,128)} fusion(f32[1024,4,2,128]{0,3,2,1:T(8,128)} %get-tuple-element.276, f32[4,512,1024,2]{2,1,3,0:T(8,128)S(1)} %get-tuple-element.258, f32[1024,4,2]{0,2,1:T(2,128)S(1)} %fusion.138, pred[1024,512]{0,1:T(8,128)(4,1)S(1)} %compare_or_fusion.2, f32[1024,4,2]{0,2,1:T(2,128)S(1)} %get-tuple-element.260, ...), kind=kOutput, calls=%fused_computation.8.clone.1 | convolution fusion | flops 1097859072 | bytes 26279936 | tf_op jit(solution)/shard_map/while/body/eval_jaxpr/nkgp,pkd->nkgd/dot_general | solution.py:166
  94.6 2.4 constant_dynamic-slice_fusion.6
  96.9 1.1 copy.285
  98.1 4.6 %fusion.137 = (f32[1024,4,2]{0,2,1:T(2,128)S(1)}, f32[4,512,1024,2]{2,1,3,0:T(8,128)S(1)}) fusion(pred[1024,512]{0,1:T(8,128)(4,1)S(1)} %compare_or_fusion.2, bf16[1024,4,2,128]{3,0,2,1:T(8,128)(2,1)} %get-tuple-element.291, bf16[1,512,4,128]{3,2,1,0:T(4,128)(2,1)} %get-tuple-element.256), kind=kOutput, calls=%fused_computation.3.clone.1 | convolution fusion | flops 1086316544 | bytes 19955712 | tf_op jit(solution)/shard_map/while/body/eval_jaxpr/nkgd,pkd->nkgp/dot_general | solution.py:154
  102.7 4.1 %fusion.139 = f32[1024,4,2]{0,2,1:T(2,128)S(1)} fusion(f32[4,512,1024,2]{2,1,3,0:T(8,128)S(1)} %get-tuple-element.258, f32[1024,4,2]{0,2,1:T(2,128)S(1)} %fusion.138, pred[1024,512]{0,1:T(8,128)(4,1)S(1)} %compare_or_fusion.2), kind=kLoop, calls=%fused_computation.5.clone.1 | loop fusion | flops 20963328 | bytes 17367040 | tf_op jit(solution)/shard_map/while/body/eval_jaxpr/reduce_sum | solution.py:165
  106.9 8.7 %bitcast_add_fusion.2 = f32[1024,4,2,128]{0,3,2,1:T(8,128)} fusion(f32[1024,4,2,128]{0,3,2,1:T(8,128)} %get-tuple-element.276, f32[4,512,1024,2]{2,1,3,0:T(8,128)S(1)} %get-tuple-element.258, f32[1024,4,2]{0,2,1:T(2,128)S(1)} %fusion.138, pred[1024,512]{0,1:T(8,128)(4,1)S(1)} %compare_or_fusion.2, f32[1024,4,2]{0,2,1:T(2,128)S(1)} %get-tuple-element.260, ...), kind=kOutput, calls=%fused_computation.8.clone.1 | convolution fusion | flops 1097859072 | bytes 26279936 | tf_op jit(solution)/shard_map/while/body/eval_jaxpr/nkgp,pkd->nkgd/dot_general | solution.py:166
  116.0 2.4 constant_dynamic-slice_fusion.6
  118.4 1.1 copy.285
  119.5 4.6 %fusion.137 = (f32[1024,4,2]{0,2,1:T(2,128)S(1)}, f32[4,512,1024,2]{2,1,3,0:T(8,128)S(1)}) fusion(pred[1024,512]{0,1:T(8,128)(4,1)S(1)} %compare_or_fusion.2, bf16[1024,4,2,128]{3,0,2,1:T(8,128)(2,1)} %get-tuple-element.291, bf16[1,512,4,128]{3,2,1,0:T(4,128)(2,1)} %get-tuple-element.256), kind=kOutput, calls=%fused_computation.3.clone.1 | convolution fusion | flops 1086316544 | bytes 19955712 | tf_op jit(solution)/shard_map/while/body/eval_jaxpr/nkgd,pkd->nkgp/dot_general | solution.py:154
  124.1 4.1 %fusion.139 = f32[1024,4,2]{0,2,1:T(2,128)S(1)} fusion(f32[4,512,1024,2]{2,1,3,0:T(8,128)S(1)} %get-tuple-element.258, f32[1024,4,2]{0,2,1:T(2,128)S(1)} %fusion.138, pred[1024,512]{0,1:T(8,128)(4,1)S(1)} %compare_or_fusion.2), kind=kLoop, calls=%fused_computation.5.clone.1 | loop fusion | flops 20963328 | bytes 17367040 | tf_op jit(solution)/shard_map/while/body/eval_jaxpr/reduce_sum | solution.py:165
  128.3 8.7 %bitcast_add_fusion.2 = f32[1024,4,2,128]{0,3,2,1:T(8,128)} fusion(f32[1024,4,2,128]{0,3,2,1:T(8,128)} %get-tuple-element.276, f32[4,512,1024,2]{2,1,3,0:T(8,128)S(1)} %get-tuple-element.258, f32[1024,4,2]{0,2,1:T(2,128)S(1)} %fusion.138, pred[1024,512]{0,1:T(8,128)(4,1)S(1)} %compare_or_fusion.2, f32[1024,4,2]{0,2,1:T(2,128)S(1)} %get-tuple-element.260, ...), kind=kOutput, calls=%fused_computation.8.clone.1 | convolution fusion | flops 1097859072 | bytes 26279936 | tf_op jit(solution)/shard_map/while/body/eval_jaxpr/nkgp,pkd->nkgd/dot_general | solution.py:166
  137.4 2.4 constant_dynamic-slice_fusion.6
  139.8 1.1 copy.285
  140.9 4.6 %fusion.137 = (f32[1024,4,2]{0,2,1:T(2,128)S(1)}, f32[4,512,1024,2]{2,1,3,0:T(8,128)S(1)}) fusion(pred[1024,512]{0,1:T(8,128)(4,1)S(1)} %compare_or_fusion.2, bf16[1024,4,2,128]{3,0,2,1:T(8,128)(2,1)} %get-tuple-element.291, bf16[1,512,4,128]{3,2,1,0:T(4,128)(2,1)} %get-tuple-element.256), kind=kOutput, calls=%fused_computation.3.clone.1 | convolution fusion | flops 1086316544 | bytes 19955712 | tf_op jit(solution)/shard_map/while/body/eval_jaxpr/nkgd,pkd->nkgp/dot_general | solution.py:154
  145.5 4.1 %fusion.139 = f32[1024,4,2]{0,2,1:T(2,128)S(1)} fusion(f32[4,512,1024,2]{2,1,3,0:T(8,128)S(1)} %get-tuple-element.258, f32[1024,4,2]{0,2,1:T(2,128)S(1)} %fusion.138, pred[1024,512]{0,1:T(8,128)(4,1)S(1)} %compare_or_fusion.2), kind=kLoop, calls=%fused_computation.5.clone.1 | loop fusion | flops 20963328 | bytes 17367040 | tf_op jit(solution)/shard_map/while/body/eval_jaxpr/reduce_sum | solution.py:165
  149.7 8.7 %bitcast_add_fusion.2 = f32[1024,4,2,128]{0,3,2,1:T(8,128)} fusion(f32[1024,4,2,128]{0,3,2,1:T(8,128)} %get-tuple-element.276, f32[4,512,1024,2]{2,1,3,0:T(8,128)S(1)} %get-tuple-element.258, f32[1024,4,2]{0,2,1:T(2,128)S(1)} %fusion.138, pred[1024,512]{0,1:T(8,128)(4,1)S(1)} %compare_or_fusion.2, f32[1024,4,2]{0,2,1:T(2,128)S(1)} %get-tuple-element.260, ...), kind=kOutput, calls=%fused_computation.8.clone.1 | convolution fusion | flops 1097859072 | bytes 26279936 | tf_op jit(solution)/shard_map/while/body/eval_jaxpr/nkgp,pkd->nkgd/dot_general | solution.py:166
  158.4 5.4 %copy.208 = f32[1024,1024]{1,0:T(8,128)} copy(f32[1024,1024]{0,1:T(8,128)} %bitcast.172) | data formatting | bytes 8388608 | tf_op jit(solution)/shard_map/reshape;reshape | solution.py:187
  163.8 59.5 %pmax.7 = bf16[1024,8]{0,1:T(8,128)(2,1)S(1)} all-reduce(bf16[1024,8]{0,1:T(8,128)(2,1)S(1)} %convert_element_type.109), channel_id=1, replica_groups=mesh['kv'=2,'seq'=16] {'seq'}, use_global_device_ids=true, to_apply=%region_13.14 | all-reduce | flops 8192 | bytes 32768 | tf_op jit(solution)/shard_map/pmax | solution.py:185
  223.3 0.9 copy.213
  224.7 1.1 mul.385
  225.8 1.0 copy-done.1
  226.9 2.2 fusion.23
  229.1 0.7 rsqrt.35
  229.8 0.7 copy.220
  230.5 0.7 reshape.346
  231.2 0.7 rsqrt.36
  232.1 1.4 copy.176
  233.5 0.8 mul.436
  234.2 0.7 mul.437
  234.9 1.4 copy.191
  236.3 2.1 convolution_convert_fusion.2
  239.1 0.9 mul.399.clone
  240.0 0.7 mul.430
  240.7 0.8 fusion.47
  241.9 0.7 mul.441
  242.6 0.8 multiply_cosine_fusion
  243.5 1.4 fusion.102
  245.6 1.1 convolution_bitcast_fusion
  247.1 0.8 fusion.43
  248.0 0.7 compare_bitcast_fusion
  248.7 0.7 broadcast_bitcast_fusion.1
  249.4 0.9 fusion.82
  250.3 1.1 add_convert_fusion.1
  251.4 25.6 %reduce-scatter.10.cloned.1.call-done = bf16[64,8]{1,0:T(8,128)(2,1)} async-done(((bf16[1024,8]{1,0:T(8,128)(2,1)}), bf16[64,8]{1,0:T(8,128)(2,1)}) %reduce-scatter.10.cloned.1.call-update) | async-done | bytes 1040
  277.0 0.8 copy.214
  278.1 63.2 %reduce-scatter.6.cloned.1.call-done = bf16[64,1024]{1,0:T(8,128)(2,1)} async-done(((bf16[1024,1024]{1,0:T(8,128)(2,1)}), bf16[64,1024]{1,0:T(8,128)(2,1)}) %reduce-scatter.6.cloned.1.call-update) | async-done | bytes 131088 | tf_op jit(solution)/shard_map/reduce_scatter | solution.py:191
  341.3 0.9 mul.425
  342.6 3.9 %convolution_convert_fusion = bf16[64,2048]{1,0:T(8,128)(2,1)} fusion(bf16[1024,2048]{1,0:T(8,128)(2,1)} %param.24, f32[8,8,8,128]{3,2,1,0:T(8,128)S(1)} %bitcast.180, f32[8,8,8,128]{3,2,1,0:T(8,128)S(1)} %bitcast.183, f32[64,1024]{1,0:T(8,128)S(1)} %reshape.350, f32[8,8,8,128]{3,2,1,0:T(8,128)S(1)} %bitcast.181, f32[8,8,8,128]{3,2,1,0:T(8,128)S(1)} %bitcast.182, ...), kind=kOutput, calls=%fused_computation.37 | convolution fusion | flops 269025280 | bytes 5898240 | tf_op jit(solution)/shard_map/dot_general | solution.py:213
  346.8 0.7 fusion.100
  347.5 9.8 %reduce-scatter.8.cloned.1.call-done = bf16[64,1024]{1,0:T(8,128)(2,1)} async-done(((bf16[64,2048]{1,0:T(8,128)(2,1)}), bf16[64,1024]{1,0:T(8,128)(2,1)}) %reduce-scatter.8.cloned.1.call-update) | async-done | bytes 131088 | tf_op jit(solution)/shard_map/reduce_scatter | solution.py:214
  357.3 1.6 add_convert_fusion
  (175 shorter events, 12.3 us)
Async XLA Ops:
  7.2 17.1 %copy-start = (bf16[2048,512]{1,0:T(8,128)(2,1)S(1)}, bf16[2048,512]{1,0:T(8,128)(2,1)}, u32[]{:S(2)}) copy-start(bf16[2048,512]{1,0:T(8,128)(2,1)} %param.21) | copy-start | bytes 6291460
  7.2 11.9 %copy-start.21 = (f32[128]{0:T(128)S(1)}, f32[128]{0:T(128)}, u32[]{:S(2)}) copy-start(f32[128]{0:T(128)} %param.25) | copy-start | bytes 1540
  7.2 12.1 %copy-start.28 = (s32[2,32]{1,0:T(2,128)S(1)}, s32[2,32]{1,0:T(2,128)}, u32[]{:S(2)}) copy-start(s32[2,32]{1,0:T(2,128)} %param.32) | copy-start | bytes 772
  7.2 13.1 %copy-start.27 = (s32[32]{0:T(128)S(1)}, s32[32]{0:T(128)}, u32[]{:S(2)}) copy-start(s32[32]{0:T(128)} %param.30) | copy-start | bytes 388
  7.2 13.1 %copy-start.26 = (s32[32]{0:T(128)S(1)}, s32[32]{0:T(128)}, u32[]{:S(2)}) copy-start(s32[32]{0:T(128)} %param.31) | copy-start | bytes 388
  7.2 13.3 %copy-start.29 = (s32[4]{0:T(128)S(1)}, s32[4]{0:T(128)}, u32[]{:S(2)}) copy-start(s32[4]{0:T(128)} %param.29) | copy-start | bytes 52
  7.2 59.4 %all-gather.2.cloned.1.call-start = ((), (), s32[]{:S(2)}) async-start(), calls=%async_computation.3 | async-start | bytes 2228224 | tf_op jit(solution)/shard_map/all_gather | solution.py:140
  7.3 14.6 %copy-start.25 = (f32[64]{0:T(128)}, f32[64]{0:T(128)S(1)}, u32[]{:S(2)}) copy-start(f32[64]{0:T(128)S(1)} %multiply_exponential_fusion) | copy-start | bytes 772
  15.5 10.3 %copy-start.3 = (bf16[64,2048]{1,0:T(8,128)(2,1)}, bf16[64,2048]{1,0:T(8,128)(2,1)S(1)}, u32[]{:S(2)}) copy-start(bf16[64,2048]{1,0:T(8,128)(2,1)S(1)} %all_gather.6) | copy-start | bytes 786436
  15.6 10.2 %copy-start.22 = (f32[64]{0:T(128)}, f32[64]{0:T(128)S(1)}, u32[]{:S(2)}) copy-start(f32[64]{0:T(128)S(1)} %add_rsqrt_fusion.2) | copy-start | bytes 772
  15.6 8.6 %copy-start.19 = (f32[2048]{0:T(1024)S(1)}, f32[2048]{0:T(1024)}, u32[]{:S(2)}) copy-start(f32[2048]{0:T(1024)} %param.19) | copy-start | bytes 24580
  18.8 7.1 %copy-start.30 = (bf16[2048,8]{0,1:T(8,128)(2,1)S(1)}, bf16[2048,8]{0,1:T(8,128)(2,1)}, u32[]{:S(2)}) copy-start(bf16[2048,8]{0,1:T(8,128)(2,1)} %param.23) | copy-start | bytes 98308
  20.3 50.7 %copy-start.15 = (f32[2,32,32]{2,1,0:T(8,128)}, f32[2,32,32]{2,1,0:T(8,128)S(1)}, u32[]{:S(2)}) copy-start(f32[2,32,32]{2,1,0:T(8,128)S(1)} %get-tuple-element.190) | copy-start | bytes 24580
  21.3 49.8 %copy-start.24 = (f32[2,32]{1,0:T(2,128)}, f32[2,32]{1,0:T(2,128)S(1)}, u32[]{:S(2)}) copy-start(f32[2,32]{1,0:T(2,128)S(1)} %get-tuple-element.186) | copy-start | bytes 772
  21.7 0.8 copy-start.16
  21.7 0.6 copy-start.14
  21.9 0.7 copy-start.7
  21.9 0.8 copy-start.9
  23.6 253.4 %reduce-scatter.10.cloned.1.call-start = ((), (), s32[]{:S(2)}) async-start(), calls=%async_computation.6 | async-start | bytes 278528
  24.8 49.5 %copy-start.5 = (f32[64,512]{1,0:T(8,128)}, f32[64,512]{1,0:T(8,128)S(1)}, u32[]{:S(2)}) copy-start(f32[64,512]{1,0:T(8,128)S(1)} %fusion.94) | copy-start | bytes 393220
  82.8 4.2 %copy-start.2 = (bf16[1,512,4,128]{1,3,2,0:T(8,128)(2,1)S(1)}, bf16[1,512,4,128]{1,3,2,0:T(8,128)(2,1)}, u32[]{:S(2)}) copy-start(bf16[1,512,4,128]{1,3,2,0:T(8,128)(2,1)} %copy.285) | copy-start | bytes 1572868 | tf_op jit(solution)/shard_map/while
  102.7 4.2 %copy-start.2 = (bf16[1,512,4,128]{1,3,2,0:T(8,128)(2,1)S(1)}, bf16[1,512,4,128]{1,3,2,0:T(8,128)(2,1)}, u32[]{:S(2)}) copy-start(bf16[1,512,4,128]{1,3,2,0:T(8,128)(2,1)} %copy.285) | copy-start | bytes 1572868 | tf_op jit(solution)/shard_map/while
  124.1 4.2 %copy-start.2 = (bf16[1,512,4,128]{1,3,2,0:T(8,128)(2,1)S(1)}, bf16[1,512,4,128]{1,3,2,0:T(8,128)(2,1)}, u32[]{:S(2)}) copy-start(bf16[1,512,4,128]{1,3,2,0:T(8,128)(2,1)} %copy.285) | copy-start | bytes 1572868 | tf_op jit(solution)/shard_map/while
  145.5 4.2 %copy-start.2 = (bf16[1,512,4,128]{1,3,2,0:T(8,128)(2,1)S(1)}, bf16[1,512,4,128]{1,3,2,0:T(8,128)(2,1)}, u32[]{:S(2)}) copy-start(bf16[1,512,4,128]{1,3,2,0:T(8,128)(2,1)} %copy.285) | copy-start | bytes 1572868 | tf_op jit(solution)/shard_map/while
  224.2 117.1 %reduce-scatter.6.cloned.1.call-start = ((), (), s32[]{:S(2)}) async-start(), calls=%async_computation.4 | async-start | bytes 2228224 | tf_op jit(solution)/shard_map/reduce_scatter | solution.py:191
  224.7 2.2 copy-start.1
  226.9 3.6 copy-start.6
  226.9 9.5 %copy-start.4 = (bf16[64,2048]{1,0:T(8,128)(2,1)S(1)}, bf16[64,2048]{1,0:T(8,128)(2,1)}, u32[]{:S(2)}) copy-start(bf16[64,2048]{1,0:T(8,128)(2,1)} %copy-done.3) | copy-start | bytes 786436
  229.0 14.5 %copy-start.8 = (f32[64,8,64]{2,0,1:T(8,128)S(1)}, f32[64,8,64]{2,0,1:T(8,128)}, u32[]{:S(2)}) copy-start(f32[64,8,64]{2,0,1:T(8,128)} %copy-done.7) | copy-start | bytes 393220
  229.0 14.5 %copy-start.10 = (f32[64,8,64]{2,0,1:T(8,128)S(1)}, f32[64,8,64]{2,0,1:T(8,128)}, u32[]{:S(2)}) copy-start(f32[64,8,64]{2,0,1:T(8,128)} %copy-done.9) | copy-start | bytes 393220
  229.0 128.3 %reduce-scatter.8.cloned.1.call-start = ((), (), s32[]{:S(2)}) async-start(), calls=%async_computation.5 | async-start | bytes 393216 | tf_op jit(solution)/shard_map/reduce_scatter | solution.py:214
  229.1 2.1 copy-start.20
  232.1 9.6 %copy-start.17 = (f32[64,128]{1,0:T(8,128)S(1)}, f32[64,128]{1,0:T(8,128)}, u32[]{:S(2)}) copy-start(f32[64,128]{1,0:T(8,128)} %copy-done.16) | copy-start | bytes 98308
  238.5 1.6 copy-start.11
  244.9 0.6 copy-start.18
  247.1 99.4 %copy-start.12 = (bf16[64,512]{1,0:T(8,128)(2,1)S(1)}, bf16[64,512]{1,0:T(8,128)(2,1)}, u32[]{:S(2)}) copy-start(bf16[64,512]{1,0:T(8,128)(2,1)} %copy-done.11) | copy-start | bytes 196612
  247.1 99.4 %copy-start.23 = (f32[2,32]{1,0:T(2,128)S(1)}, f32[2,32]{1,0:T(2,128)}, u32[]{:S(2)}) copy-start(f32[2,32]{1,0:T(2,128)} %get-tuple-element.185) | copy-start | bytes 772
  251.4 105.9 %copy-start.13 = (bf16[64,1024]{1,0:T(8,128)(2,1)S(1)}, bf16[64,1024]{1,0:T(8,128)(2,1)}, u32[]{:S(2)}) copy-start(bf16[64,1024]{1,0:T(8,128)(2,1)} %param.18) | copy-start | bytes 393220
Sparse Core Ops, SparseCore 0:
  23.7 42.8 all-gather.1
  224.3 52.5 reduce-scatter.9
  280.7 60.5 reduce-scatter.5
  346.6 10.6 reduce-scatter.7
where the time goes:
time: 367 us; the launch traced here: 365 us
  waiting for transfers between devices  139 us (38%)
  blocking collectives  66.8 us (18%)
  matrix products  66.7 us (18%)
  local copies, waits for them, and re-layouts  47.5 us (13%)
  other arithmetic  30.8 us (8%)
  between operations  14.5 us (4%)
    reduce_scatter x1, waiting for transfers between devices, body(): lax.psum_scatter(scaled_num.astype(jnp.bfloat16), 'seq', scatter_dimensio...  63.2 us
    pmax x1, blocking collectives, body(): lax.pmax(part_max.astype(jnp.bfloat16), 'seq').astype(part_max.dtype)  59.5 us
    all_gather x1, waiting for transfers between devices, body(): query_piece = lax.all_gather(query_flat, 'seq', axis=0, tiled=True)  39.9 us
    dot_general x4, matrix products, visit(): jnp.einsum('nkgp,pkd->nkgd', weights.astype(jnp.bfloat16), values_block,...  33.2 us
    unnamed x5, waiting for transfers between devices  25.6 us
    dot_general x4, matrix products, visit(): jnp.einsum('nkgd,pkd->nkgp', grouped, keys_block, preferred_element_type=...  18.3 us
    reduce_sum x4, other arithmetic, visit(): run_sum = run_sum * factor + jnp.sum(weights, axis=-1)  16.3 us
    dynamic_slice x12, local copies, waits for them, and re-layouts, body(): lax.scan(visit, start_state, (key_blocks, value_blocks, segment_blocks))  14 us
  transfers between devices with their start and end apart: 4, of which 4 were waited for; matrix products, arithmetic and copies ran while one was open for 8% of the time, Pallas kernels for 0%

commit v1 on v0

--- a/solution.py
+++ b/solution.py
@@ -7,6 +7,15 @@
 EPSILON = 1e-06
 ROPE_BASE = 1000000.0
 NEGATIVE = -1e30
+
+
+def tell_seats_all_in(mine, in_dim):
+    mine = jnp.moveaxis(mine, 0, in_dim)
+    g_now = mine.shape
+    value_now = mine.reshape(
+        *g_now[:in_dim], g_now[in_dim] * g_now[in_dim + 1], *g_now[in_dim + 2 :]
+    )
+    return value_now
 
 
 def rms_scale(values, scales):
@@ -137,7 +146,25 @@
     value_blocks = pooled_cache_values.reshape(block_count, block_len, local_kv, head_width)
     segment_blocks = slot_segment.reshape(block_count, block_len)
     query_flat = query.reshape(local_tok, local_heads * head_width)
-    query_piece = lax.all_gather(query_flat, "seq", axis=0, tiled=True)
+    count_all = jax.lax.axis_size("seq")
+    fields = []
+    for it in range(count_all):
+        fields.append((it, (it + 1) % count_all))
+    blocks_here = []
+    for at, c in fields:
+        blocks_here.append((c, at))
+    a_now, big = ([], [])
+    for idx in range(count_all - 1):
+        if idx % 2 == 0:
+            a_now.append(jax.lax.ppermute(a_now[-1] if a_now else query_flat, "seq", fields))
+        else:
+            big.append(jax.lax.ppermute(big[-1] if big else query_flat, "seq", blocks_here))
+    reply = jnp.stack([*a_now[::-1], query_flat, *big])
+    found_now = len(a_now)
+    f_next = jax.lax.axis_index("seq")
+    upper = f_next - found_now
+    reply = reply[(jnp.arange(count_all) - upper) % count_all]
+    query_piece = tell_seats_all_in(reply, 0)
     row_ids = jnp.arange(query_piece.shape[0], dtype=jnp.int32)
     owners = row_ids // tree
     count = query_piece.shape[0]

time: 367 us -> 392 us (1.068)
  starting transfers between devices: 0.34 us -> 31 us
  other arithmetic: 30.8 us -> 26.4 us
    all_gather x1 -> x0, waiting for transfers between devices: 39.9 us -> none  [body(): query_piece = lax.all_gather(query_flat, 'seq', axis=0, tiled=True)]
    ppermute x0 -> x15, starting transfers between devices: none -> 30.6 us  [the longest x7 30.6 us: body(): jax.lax.ppermute(big[-1] if big else query_flat, 'seq', blocks_here)]
    ppermute x0 -> x15, waiting for transfers between devices: none -> 26.4 us  [the longest x8 26.4 us: body(): jax.lax.ppermute(a_now[-1] if a_now else query_flat, 'seq', fields)]
    unnamed x5 -> x4, waiting for transfers between devices: 25.6 us -> 41.7 us
    unnamed x66 -> x89, local copies, waits for them, and re-layouts: 8.05 us -> 16.2 us
    reshape x1 -> x0, local copies, waits for them, and re-layouts: 4.48 us -> none  [body(): grouped = query_piece.reshape(count, local_kv, per_kv, head_width)]
  transfers between devices with their start and end apart: 4 -> 18, of which waited for: 4 -> 11; matrix products, arithmetic and copies ran while one was open for 8% -> 6% of each run, Pallas kernels for 0% -> 0%
where the time goes in v1:
time: 392 us
  waiting for transfers between devices  141 us (36%)
  blocking collectives  65 us (17%)
  matrix products  63.4 us (16%)
  local copies, waits for them, and re-layouts  49.8 us (13%)
  starting transfers between devices  31 us (8%)
  other arithmetic  26.4 us (7%)
  between operations  14.6 us (4%)
    reduce_scatter x1, waiting for transfers between devices, body(): lax.psum_scatter(scaled_num.astype(jnp.bfloat16), 'seq', scatter_dimensio...  63.3 us
    pmax x1, blocking collectives, body(): lax.pmax(part_max.astype(jnp.bfloat16), 'seq').astype(part_max.dtype)  57.6 us
    unnamed x4, waiting for transfers between devices  41.7 us
    dot_general x4, matrix products, visit(): jnp.einsum('nkgp,pkd->nkgd', weights.astype(jnp.bfloat16), values_block,...  33.3 us
    ppermute x7, starting transfers between devices, body(): jax.lax.ppermute(big[-1] if big else query_flat, 'seq', blocks_here)  30.6 us
    ppermute x8, waiting for transfers between devices, body(): jax.lax.ppermute(a_now[-1] if a_now else query_flat, 'seq', fields)  26.4 us
    dot_general x4, matrix products, visit(): jnp.einsum('nkgd,pkd->nkgp', grouped, keys_block, preferred_element_type=...  17.3 us
    reduce_sum x4, other arithmetic, visit(): run_sum = run_sum * factor + jnp.sum(weights, axis=-1)  16.3 us
  transfers between devices with their start and end apart: 18, of which 11 were waited for; matrix products, arithmetic and copies ran while one was open for 6% of the time, Pallas kernels for 0%

profile of v1, /device:TPU:0, one launch (start us, length us, event | category | flops | bytes accessed | tf_op | source)
XLA Modules:
  0.0 391.7 jit_solution(12325708596908857779)
XLA Ops:
  7.3 0.8 broadcast_bitcast_fusion
  8.1 7.4 %all_gather.3 = bf16[64,2048]{1,0:T(8,128)(2,1)S(1)} all-gather(bf16[64,1024]{1,0:T(8,128)(2,1)} %param.18), channel_id=1, replica_groups=mesh['kv'=2,'seq'=16] {'kv'}, dimensions={1}, use_global_device_ids=true | all-gather | bytes 393216 | tf_op jit(solution)/shard_map/all_gather | solution.py:93
  15.7 3.1 fusion.98
  23.2 3.4 collective-permute-start.8
  27.5 0.9 fusion.28
  28.4 5.3 %collective-permute-done = bf16[64,1024]{1,0:T(8,128)(2,1)S(1)} collective-permute-done((bf16[64,1024]{1,0:T(8,128)(2,1)S(1)}, bf16[64,1024]{1,0:T(8,128)(2,1)S(1)}, u32[]{:S(2)}, u32[]{:S(2)}) %collective-permute-start) | collective-permute-done | bytes 131104 | tf_op jit(solution)/shard_map/ppermute | solution.py:159
  34.2 6.6 %collective-permute-done.1 = bf16[64,1024]{1,0:T(8,128)(2,1)S(1)} collective-permute-done((bf16[64,1024]{1,0:T(8,128)(2,1)S(1)}, bf16[64,1024]{1,0:T(8,128)(2,1)S(1)}, u32[]{:S(2)}, u32[]{:S(2)}) %collective-permute-start.1) | collective-permute-done | bytes 131104 | tf_op jit(solution)/shard_map/ppermute | solution.py:159
  40.9 4.4 %collective-permute-start.9 = (bf16[64,1024]{1,0:T(8,128)(2,1)S(1)}, bf16[64,1024]{1,0:T(8,128)(2,1)S(1)}, u32[]{:S(2)}, u32[]{:S(2)}) collective-permute-start(bf16[64,1024]{1,0:T(8,128)(2,1)S(1)} %collective-permute-done.8), channel_id=1, source_target_pairs={{1,0},{2,1},{3,2},{4,3},{5,4},{6,5},{7,6},{8,7},{9,8},{10,9},{11,1... | collective-permute-start | bytes 393224 | tf_op jit(solution)/shard_map/ppermute | solution.py:161
  45.3 2.7 collective-permute-done.2
  48.2 4.5 %collective-permute-start.10 = (bf16[64,1024]{1,0:T(8,128)(2,1)S(1)}, bf16[64,1024]{1,0:T(8,128)(2,1)S(1)}, u32[]{:S(2)}, u32[]{:S(2)}) collective-permute-start(bf16[64,1024]{1,0:T(8,128)(2,1)S(1)} %collective-permute-done.9), channel_id=1, source_target_pairs={{1,0},{2,1},{3,2},{4,3},{5,4},{6,5},{7,6},{8,7},{9,8},{10,9},{11,1... | collective-permute-start | bytes 393224 | tf_op jit(solution)/shard_map/ppermute | solution.py:161
  52.7 2.6 collective-permute-done.3
  55.2 4.6 %collective-permute-start.11 = (bf16[64,1024]{1,0:T(8,128)(2,1)S(1)}, bf16[64,1024]{1,0:T(8,128)(2,1)S(1)}, u32[]{:S(2)}, u32[]{:S(2)}) collective-permute-start(bf16[64,1024]{1,0:T(8,128)(2,1)S(1)} %collective-permute-done.10), channel_id=1, source_target_pairs={{1,0},{2,1},{3,2},{4,3},{5,4},{6,5},{7,6},{8,7},{9,8},{10,9},{11,1... | collective-permute-start | bytes 393224 | tf_op jit(solution)/shard_map/ppermute | solution.py:161
  59.8 2.6 collective-permute-done.4
  62.5 4.5 %collective-permute-start.12 = (bf16[64,1024]{1,0:T(8,128)(2,1)S(1)}, bf16[64,1024]{1,0:T(8,128)(2,1)S(1)}, u32[]{:S(2)}, u32[]{:S(2)}) collective-permute-start(bf16[64,1024]{1,0:T(8,128)(2,1)S(1)} %collective-permute-done.11), channel_id=1, source_target_pairs={{1,0},{2,1},{3,2},{4,3},{5,4},{6,5},{7,6},{8,7},{9,8},{10,9},{11,1... | collective-permute-start | bytes 393224 | tf_op jit(solution)/shard_map/ppermute | solution.py:161
  67.0 2.6 collective-permute-done.5
  69.8 4.5 %collective-permute-start.13 = (bf16[64,1024]{1,0:T(8,128)(2,1)S(1)}, bf16[64,1024]{1,0:T(8,128)(2,1)S(1)}, u32[]{:S(2)}, u32[]{:S(2)}) collective-permute-start(bf16[64,1024]{1,0:T(8,128)(2,1)S(1)} %collective-permute-done.12), channel_id=1, source_target_pairs={{1,0},{2,1},{3,2},{4,3},{5,4},{6,5},{7,6},{8,7},{9,8},{10,9},{11,1... | collective-permute-start | bytes 393224 | tf_op jit(solution)/shard_map/ppermute | solution.py:161
  74.3 2.5 collective-permute-done.6
  76.9 0.7 copy.177
  77.5 4.7 %collective-permute-start.14 = (bf16[64,1024]{1,0:T(8,128)(2,1)S(1)}, bf16[64,1024]{1,0:T(8,128)(2,1)S(1)}, u32[]{:S(2)}, u32[]{:S(2)}) collective-permute-start(bf16[64,1024]{1,0:T(8,128)(2,1)S(1)} %collective-permute-done.13), channel_id=1, source_target_pairs={{1,0},{2,1},{3,2},{4,3},{5,4},{6,5},{7,6},{8,7},{9,8},{10,9},{11,1... | collective-permute-start | bytes 393224 | tf_op jit(solution)/shard_map/ppermute | solution.py:161
  82.2 1.7 collective-permute-done.7
  83.9 0.7 bitcast_dynamic-update-slice_fusion.15
  85.9 0.7 bitcast_dynamic-update-slice_fusion.12
  86.5 0.7 bitcast_dynamic-update-slice_fusion.11
  87.2 0.7 bitcast_dynamic-update-slice_fusion.10
  90.6 0.7 bitcast_dynamic-update-slice_fusion.5
  91.9 0.7 bitcast_dynamic-update-slice_fusion.3
  92.6 0.7 bitcast_dynamic-update-slice_fusion.2
  94.6 2.3 gather_fusion
  96.8 2.7 reshape_reshape.12
  99.6 1.9 copy.172
  101.4 85.5 %while.15 = (s32[]{:T(128)}, f32[1024,4,2]{0,2,1:T(2,128)S(1)}, f32[1024,4,2]{0,2,1:T(2,128)S(1)}, f32[1024,4,2,128]{0,3,2,1:T(8,128)}, s32[4,512]{1,0:T(4,128)S...) while((s32[]{:T(128)}, f32[1024,4,2]{0,2,1:T(2,128)S(1)}, ...), condition=%wide.region_12.13_spmd.clone, body=%wide.region_9.12_spmd.clone.sunk | while | flops 2206780416 | bytes 69814488 | solution.py:206
  102.5 2.4 constant_dynamic-slice_fusion.6
  104.8 1.1 copy.285
  105.9 4.3 %fusion.139 = (f32[1024,4,2]{0,2,1:T(2,128)S(1)}, f32[4,512,1024,2]{2,1,3,0:T(8,128)S(1)}) fusion(pred[1024,512]{0,1:T(8,128)(4,1)S(1)} %compare_or_fusion.2, bf16[1024,4,2,128]{3,0,2,1:T(8,128)(2,1)S(1)} %get-tuple-element.291, bf16[1,512,4,128]{3,2,1,0:T(4,128)(2,1)} %get-tuple-element.256), kind=kOutput, calls=%fused_computation.4.clone.1 | convolution fusion | flops 1086316544 | bytes 19955712 | tf_op jit(solution)/shard_map/while/body/eval_jaxpr/nkgd,pkd->nkgp/dot_general | solution.py:181
  110.3 4.1 %fusion.141 = f32[1024,4,2]{0,2,1:T(2,128)S(1)} fusion(f32[4,512,1024,2]{2,1,3,0:T(8,128)S(1)} %get-tuple-element.258, f32[1024,4,2]{0,2,1:T(2,128)S(1)} %fusion.140, pred[1024,512]{0,1:T(8,128)(4,1)S(1)} %compare_or_fusion.2), kind=kLoop, calls=%fused_computation.6.clone.1 | loop fusion | flops 20963328 | bytes 17367040 | tf_op jit(solution)/shard_map/while/body/eval_jaxpr/reduce_sum | solution.py:192
  114.5 7.1 %bitcast_add_fusion.2 = f32[1024,4,2,128]{0,3,2,1:T(8,128)} fusion(f32[1024,4,2,128]{0,3,2,1:T(8,128)} %get-tuple-element.276, f32[4,512,1024,2]{2,1,3,0:T(8,128)S(1)} %get-tuple-element.258, f32[1024,4,2]{0,2,1:T(2,128)S(1)} %fusion.140, pred[1024,512]{0,1:T(8,128)(4,1)S(1)} %compare_or_fusion.2, f32[1024,4,2]{0,2,1:T(2,128)S(1)} %get-tuple-element.260, ...), kind=kOutput, calls=%fused_computation.9.clone.1 | convolution fusion | flops 1097859072 | bytes 26279936 | tf_op jit(solution)/shard_map/while/body/eval_jaxpr/nkgp,pkd->nkgd/dot_general | solution.py:193
  122.7 2.4 constant_dynamic-slice_fusion.6
  125.0 1.1 copy.285
  126.2 4.3 %fusion.139 = (f32[1024,4,2]{0,2,1:T(2,128)S(1)}, f32[4,512,1024,2]{2,1,3,0:T(8,128)S(1)}) fusion(pred[1024,512]{0,1:T(8,128)(4,1)S(1)} %compare_or_fusion.2, bf16[1024,4,2,128]{3,0,2,1:T(8,128)(2,1)S(1)} %get-tuple-element.291, bf16[1,512,4,128]{3,2,1,0:T(4,128)(2,1)} %get-tuple-element.256), kind=kOutput, calls=%fused_computation.4.clone.1 | convolution fusion | flops 1086316544 | bytes 19955712 | tf_op jit(solution)/shard_map/while/body/eval_jaxpr/nkgd,pkd->nkgp/dot_general | solution.py:181
  130.5 4.1 %fusion.141 = f32[1024,4,2]{0,2,1:T(2,128)S(1)} fusion(f32[4,512,1024,2]{2,1,3,0:T(8,128)S(1)} %get-tuple-element.258, f32[1024,4,2]{0,2,1:T(2,128)S(1)} %fusion.140, pred[1024,512]{0,1:T(8,128)(4,1)S(1)} %compare_or_fusion.2), kind=kLoop, calls=%fused_computation.6.clone.1 | loop fusion | flops 20963328 | bytes 17367040 | tf_op jit(solution)/shard_map/while/body/eval_jaxpr/reduce_sum | solution.py:192
  134.7 8.7 %bitcast_add_fusion.2 = f32[1024,4,2,128]{0,3,2,1:T(8,128)} fusion(f32[1024,4,2,128]{0,3,2,1:T(8,128)} %get-tuple-element.276, f32[4,512,1024,2]{2,1,3,0:T(8,128)S(1)} %get-tuple-element.258, f32[1024,4,2]{0,2,1:T(2,128)S(1)} %fusion.140, pred[1024,512]{0,1:T(8,128)(4,1)S(1)} %compare_or_fusion.2, f32[1024,4,2]{0,2,1:T(2,128)S(1)} %get-tuple-element.260, ...), kind=kOutput, calls=%fused_computation.9.clone.1 | convolution fusion | flops 1097859072 | bytes 26279936 | tf_op jit(solution)/shard_map/while/body/eval_jaxpr/nkgp,pkd->nkgd/dot_general | solution.py:193
  144.4 2.4 constant_dynamic-slice_fusion.6
  146.8 1.1 copy.285
  147.9 4.3 %fusion.139 = (f32[1024,4,2]{0,2,1:T(2,128)S(1)}, f32[4,512,1024,2]{2,1,3,0:T(8,128)S(1)}) fusion(pred[1024,512]{0,1:T(8,128)(4,1)S(1)} %compare_or_fusion.2, bf16[1024,4,2,128]{3,0,2,1:T(8,128)(2,1)S(1)} %get-tuple-element.291, bf16[1,512,4,128]{3,2,1,0:T(4,128)(2,1)} %get-tuple-element.256), kind=kOutput, calls=%fused_computation.4.clone.1 | convolution fusion | flops 1086316544 | bytes 19955712 | tf_op jit(solution)/shard_map/while/body/eval_jaxpr/nkgd,pkd->nkgp/dot_general | solution.py:181
  152.3 4.1 %fusion.141 = f32[1024,4,2]{0,2,1:T(2,128)S(1)} fusion(f32[4,512,1024,2]{2,1,3,0:T(8,128)S(1)} %get-tuple-element.258, f32[1024,4,2]{0,2,1:T(2,128)S(1)} %fusion.140, pred[1024,512]{0,1:T(8,128)(4,1)S(1)} %compare_or_fusion.2), kind=kLoop, calls=%fused_computation.6.clone.1 | loop fusion | flops 20963328 | bytes 17367040 | tf_op jit(solution)/shard_map/while/body/eval_jaxpr/reduce_sum | solution.py:192
  156.5 8.7 %bitcast_add_fusion.2 = f32[1024,4,2,128]{0,3,2,1:T(8,128)} fusion(f32[1024,4,2,128]{0,3,2,1:T(8,128)} %get-tuple-element.276, f32[4,512,1024,2]{2,1,3,0:T(8,128)S(1)} %get-tuple-element.258, f32[1024,4,2]{0,2,1:T(2,128)S(1)} %fusion.140, pred[1024,512]{0,1:T(8,128)(4,1)S(1)} %compare_or_fusion.2, f32[1024,4,2]{0,2,1:T(2,128)S(1)} %get-tuple-element.260, ...), kind=kOutput, calls=%fused_computation.9.clone.1 | convolution fusion | flops 1097859072 | bytes 26279936 | tf_op jit(solution)/shard_map/while/body/eval_jaxpr/nkgp,pkd->nkgd/dot_general | solution.py:193
  166.2 2.4 constant_dynamic-slice_fusion.6
  168.6 1.1 copy.285
  169.7 4.3 %fusion.139 = (f32[1024,4,2]{0,2,1:T(2,128)S(1)}, f32[4,512,1024,2]{2,1,3,0:T(8,128)S(1)}) fusion(pred[1024,512]{0,1:T(8,128)(4,1)S(1)} %compare_or_fusion.2, bf16[1024,4,2,128]{3,0,2,1:T(8,128)(2,1)S(1)} %get-tuple-element.291, bf16[1,512,4,128]{3,2,1,0:T(4,128)(2,1)} %get-tuple-element.256), kind=kOutput, calls=%fused_computation.4.clone.1 | convolution fusion | flops 1086316544 | bytes 19955712 | tf_op jit(solution)/shard_map/while/body/eval_jaxpr/nkgd,pkd->nkgp/dot_general | solution.py:181
  174.1 4.1 %fusion.141 = f32[1024,4,2]{0,2,1:T(2,128)S(1)} fusion(f32[4,512,1024,2]{2,1,3,0:T(8,128)S(1)} %get-tuple-element.258, f32[1024,4,2]{0,2,1:T(2,128)S(1)} %fusion.140, pred[1024,512]{0,1:T(8,128)(4,1)S(1)} %compare_or_fusion.2), kind=kLoop, calls=%fused_computation.6.clone.1 | loop fusion | flops 20963328 | bytes 17367040 | tf_op jit(solution)/shard_map/while/body/eval_jaxpr/reduce_sum | solution.py:192
  178.2 8.7 %bitcast_add_fusion.2 = f32[1024,4,2,128]{0,3,2,1:T(8,128)} fusion(f32[1024,4,2,128]{0,3,2,1:T(8,128)} %get-tuple-element.276, f32[4,512,1024,2]{2,1,3,0:T(8,128)S(1)} %get-tuple-element.258, f32[1024,4,2]{0,2,1:T(2,128)S(1)} %fusion.140, pred[1024,512]{0,1:T(8,128)(4,1)S(1)} %compare_or_fusion.2, f32[1024,4,2]{0,2,1:T(2,128)S(1)} %get-tuple-element.260, ...), kind=kOutput, calls=%fused_computation.9.clone.1 | convolution fusion | flops 1097859072 | bytes 26279936 | tf_op jit(solution)/shard_map/while/body/eval_jaxpr/nkgp,pkd->nkgd/dot_general | solution.py:193
  187.0 5.4 %copy.208 = f32[1024,1024]{1,0:T(8,128)} copy(f32[1024,1024]{0,1:T(8,128)} %bitcast.206) | data formatting | bytes 8388608 | tf_op jit(solution)/shard_map/reshape;reshape | solution.py:214
  192.4 57.6 %pmax.7 = bf16[1024,8]{0,1:T(8,128)(2,1)S(1)} all-reduce(bf16[1024,8]{0,1:T(8,128)(2,1)S(1)} %convert_element_type.114), channel_id=1, replica_groups=mesh['kv'=2,'seq'=16] {'seq'}, use_global_device_ids=true, to_apply=%region_13.14 | all-reduce | flops 8192 | bytes 32768 | tf_op jit(solution)/shard_map/pmax | solution.py:212
  250.1 0.8 copy.213
  251.2 1.1 mul.393
  252.4 1.0 copy-done.2
  253.4 2.2 fusion.23
  257.2 2.2 convolution_convert_fusion.2
  262.1 41.7 %reduce-scatter.10.cloned.1.call-done = bf16[64,8]{1,0:T(8,128)(2,1)} async-done(((bf16[1024,8]{1,0:T(8,128)(2,1)}), bf16[64,8]{1,0:T(8,128)(2,1)}) %reduce-scatter.10.cloned.1.call-update) | async-done | bytes 1040
  303.8 0.8 copy.214
  304.9 63.3 %reduce-scatter.6.cloned.1.call-done = bf16[64,1024]{1,0:T(8,128)(2,1)} async-done(((bf16[1024,1024]{1,0:T(8,128)(2,1)}), bf16[64,1024]{1,0:T(8,128)(2,1)}) %reduce-scatter.6.cloned.1.call-update) | async-done | bytes 131088 | tf_op jit(solution)/shard_map/reduce_scatter | solution.py:218
  368.7 4.0 %convolution_convert_fusion = bf16[64,2048]{1,0:T(8,128)(2,1)} fusion(bf16[1024,2048]{1,0:T(8,128)(2,1)} %param.24, f32[8,8,8,128]{3,2,1,0:T(8,128)S(1)} %bitcast.214, f32[8,8,8,128]{3,2,1,0:T(8,128)S(1)} %bitcast.217, f32[64,1024]{1,0:T(8,128)S(1)} %reshape.417, f32[8,8,8,128]{3,2,1,0:T(8,128)S(1)} %bitcast.215, f32[8,8,8,128]{3,2,1,0:T(8,128)S(1)} %bitcast.216, ...), kind=kOutput, calls=%fused_computation.38 | convolution fusion | flops 269025280 | bytes 5898240 | tf_op jit(solution)/shard_map/dot_general | solution.py:240
  373.8 9.8 %reduce-scatter.8.cloned.1.call-done = bf16[64,1024]{1,0:T(8,128)(2,1)} async-done(((bf16[64,2048]{1,0:T(8,128)(2,1)}), bf16[64,1024]{1,0:T(8,128)(2,1)}) %reduce-scatter.8.cloned.1.call-update) | async-done | bytes 131088 | tf_op jit(solution)/shard_map/reduce_scatter | solution.py:241
  383.6 1.6 add_convert_fusion
  (245 shorter events, 22.9 us)
Async XLA Ops:
  7.2 19.7 %copy-start = (bf16[2048,512]{1,0:T(8,128)(2,1)S(1)}, bf16[2048,512]{1,0:T(8,128)(2,1)}, u32[]{:S(2)}) copy-start(bf16[2048,512]{1,0:T(8,128)(2,1)} %param.21) | copy-start | bytes 6291460
  7.2 296.6 %reduce-scatter.10.cloned.1.call-start = ((), (), s32[]{:S(2)}) async-start(), calls=%async_computation.5 | async-start | bytes 278528
  7.2 14.2 %copy-start.29 = (f32[64]{0:T(128)}, f32[64]{0:T(128)S(1)}, u32[]{:S(2)}) copy-start(f32[64]{0:T(128)S(1)} %multiply_exponential_fusion) | copy-start | bytes 772
  15.4 12.0 %copy-start.4 = (bf16[64,2048]{1,0:T(8,128)(2,1)}, bf16[64,2048]{1,0:T(8,128)(2,1)S(1)}, u32[]{:S(2)}) copy-start(bf16[64,2048]{1,0:T(8,128)(2,1)S(1)} %all_gather.3) | copy-start | bytes 786436
  15.6 11.9 %copy-start.23 = (f32[64]{0:T(128)}, f32[64]{0:T(128)S(1)}, u32[]{:S(2)}) copy-start(f32[64]{0:T(128)S(1)} %add_rsqrt_fusion.2) | copy-start | bytes 772
  15.6 3.5 copy-start.20
  15.6 3.7 copy-start.33
  15.6 4.7 %copy-start.31 = (s32[32]{0:T(128)S(1)}, s32[32]{0:T(128)}, u32[]{:S(2)}) copy-start(s32[32]{0:T(128)} %param.31) | copy-start | bytes 388
  15.6 4.7 %copy-start.32 = (s32[32]{0:T(128)S(1)}, s32[32]{0:T(128)}, u32[]{:S(2)}) copy-start(s32[32]{0:T(128)} %param.30) | copy-start | bytes 388
  15.6 4.9 %copy-start.34 = (s32[4]{0:T(128)S(1)}, s32[4]{0:T(128)}, u32[]{:S(2)}) copy-start(s32[4]{0:T(128)} %param.29) | copy-start | bytes 52
  19.1 7.8 %copy-start.15 = (f32[2048]{0:T(1024)S(1)}, f32[2048]{0:T(1024)}, u32[]{:S(2)}) copy-start(f32[2048]{0:T(1024)} %param.19) | copy-start | bytes 24580
  21.3 0.6 copy-start.26
  22.0 5.5 %copy-start.13 = (f32[64,128]{1,0:T(8,128)}, f32[64,128]{1,0:T(8,128)S(1)}, u32[]{:S(2)}) copy-start(f32[64,128]{1,0:T(8,128)S(1)} %pad_maximum_fusion.1) | copy-start | bytes 98308
  22.2 0.7 copy-start.8
  22.2 0.9 copy-start.10
  22.4 5.1 %copy-start.35 = (bf16[2048,8]{0,1:T(8,128)(2,1)S(1)}, bf16[2048,8]{0,1:T(8,128)(2,1)}, u32[]{:S(2)}) copy-start(bf16[2048,8]{0,1:T(8,128)(2,1)} %param.23) | copy-start | bytes 98308
  23.2 17.8 %collective-permute-start.8 = (bf16[64,1024]{1,0:T(8,128)(2,1)S(1)}, bf16[64,1024]{1,0:T(8,128)(2,1)S(1)}, u32[]{:S(2)}, u32[]{:S(2)}) collective-permute-start(bf16[64,1024]{1,0:T(8,128)(2,1)S(1)} %fusion.35), channel_id=1, source_target_pairs={{1,0},{2,1},{3,2},{4,3},{5,4},{6,5},{7,6},{8,7},{9,8},{10,9},{11,1... | collective-permute-start | bytes 393224 | tf_op jit(solution)/shard_map/ppermute | solution.py:161
  26.5 7.1 %collective-permute-start = (bf16[64,1024]{1,0:T(8,128)(2,1)S(1)}, bf16[64,1024]{1,0:T(8,128)(2,1)S(1)}, u32[]{:S(2)}, u32[]{:S(2)}) collective-permute-start(bf16[64,1024]{1,0:T(8,128)(2,1)S(1)} %fusion.35), channel_id=1, source_target_pairs={{0,1},{1,2},{2,3},{3,4},{4,5},{5,6},{6,7},{7,8},{8,9},{9,10},{10,1... | collective-permute-start | bytes 393224 | tf_op jit(solution)/shard_map/ppermute | solution.py:159
  27.5 64.4 %copy-start.6 = (f32[64,512]{1,0:T(8,128)}, f32[64,512]{1,0:T(8,128)S(1)}, u32[]{:S(2)}) copy-start(f32[64,512]{1,0:T(8,128)S(1)} %fusion.96) | copy-start | bytes 393220
  33.6 7.2 %collective-permute-start.1 = (bf16[64,1024]{1,0:T(8,128)(2,1)S(1)}, bf16[64,1024]{1,0:T(8,128)(2,1)S(1)}, u32[]{:S(2)}, u32[]{:S(2)}) collective-permute-start(bf16[64,1024]{1,0:T(8,128)(2,1)S(1)} %collective-permute-done), channel_id=1, source_target_pairs={{0,1},{1,2},{2,3},{3,4},{4,5},{5,6},{6,7},{7,8},{8,9},{9,10},{10,1... | collective-permute-start | bytes 393224 | tf_op jit(solution)/shard_map/ppermute | solution.py:159
  40.8 7.2 %collective-permute-start.2 = (bf16[64,1024]{1,0:T(8,128)(2,1)S(1)}, bf16[64,1024]{1,0:T(8,128)(2,1)S(1)}, u32[]{:S(2)}, u32[]{:S(2)}) collective-permute-start(bf16[64,1024]{1,0:T(8,128)(2,1)S(1)} %collective-permute-done.1), channel_id=1, source_target_pairs={{0,1},{1,2},{2,3},{3,4},{4,5},{5,6},{6,7},{7,8},{8,9},{9,10},{10,1... | collective-permute-start | bytes 393224 | tf_op jit(solution)/shard_map/ppermute | solution.py:159
  40.9 7.2 %collective-permute-start.9 = (bf16[64,1024]{1,0:T(8,128)(2,1)S(1)}, bf16[64,1024]{1,0:T(8,128)(2,1)S(1)}, u32[]{:S(2)}, u32[]{:S(2)}) collective-permute-start(bf16[64,1024]{1,0:T(8,128)(2,1)S(1)} %collective-permute-done.8), channel_id=1, source_target_pairs={{1,0},{2,1},{3,2},{4,3},{5,4},{6,5},{7,6},{8,7},{9,8},{10,9},{11,1... | collective-permute-start | bytes 393224 | tf_op jit(solution)/shard_map/ppermute | solution.py:161
  48.0 7.2 %collective-permute-start.3 = (bf16[64,1024]{1,0:T(8,128)(2,1)S(1)}, bf16[64,1024]{1,0:T(8,128)(2,1)S(1)}, u32[]{:S(2)}, u32[]{:S(2)}) collective-permute-start(bf16[64,1024]{1,0:T(8,128)(2,1)S(1)} %collective-permute-done.2), channel_id=1, source_target_pairs={{0,1},{1,2},{2,3},{3,4},{4,5},{5,6},{6,7},{7,8},{8,9},{9,10},{10,1... | collective-permute-start | bytes 393224 | tf_op jit(solution)/shard_map/ppermute | solution.py:159
  48.2 7.1 %collective-permute-start.10 = (bf16[64,1024]{1,0:T(8,128)(2,1)S(1)}, bf16[64,1024]{1,0:T(8,128)(2,1)S(1)}, u32[]{:S(2)}, u32[]{:S(2)}) collective-permute-start(bf16[64,1024]{1,0:T(8,128)(2,1)S(1)} %collective-permute-done.9), channel_id=1, source_target_pairs={{1,0},{2,1},{3,2},{4,3},{5,4},{6,5},{7,6},{8,7},{9,8},{10,9},{11,1... | collective-permute-start | bytes 393224 | tf_op jit(solution)/shard_map/ppermute | solution.py:161
  55.2 7.2 %collective-permute-start.4 = (bf16[64,1024]{1,0:T(8,128)(2,1)S(1)}, bf16[64,1024]{1,0:T(8,128)(2,1)S(1)}, u32[]{:S(2)}, u32[]{:S(2)}) collective-permute-start(bf16[64,1024]{1,0:T(8,128)(2,1)S(1)} %collective-permute-done.3), channel_id=1, source_target_pairs={{0,1},{1,2},{2,3},{3,4},{4,5},{5,6},{6,7},{7,8},{8,9},{9,10},{10,1... | collective-permute-start | bytes 393224 | tf_op jit(solution)/shard_map/ppermute | solution.py:159
  55.2 7.3 %collective-permute-start.11 = (bf16[64,1024]{1,0:T(8,128)(2,1)S(1)}, bf16[64,1024]{1,0:T(8,128)(2,1)S(1)}, u32[]{:S(2)}, u32[]{:S(2)}) collective-permute-start(bf16[64,1024]{1,0:T(8,128)(2,1)S(1)} %collective-permute-done.10), channel_id=1, source_target_pairs={{1,0},{2,1},{3,2},{4,3},{5,4},{6,5},{7,6},{8,7},{9,8},{10,9},{11,1... | collective-permute-start | bytes 393224 | tf_op jit(solution)/shard_map/ppermute | solution.py:161
  62.4 7.2 %collective-permute-start.5 = (bf16[64,1024]{1,0:T(8,128)(2,1)S(1)}, bf16[64,1024]{1,0:T(8,128)(2,1)S(1)}, u32[]{:S(2)}, u32[]{:S(2)}) collective-permute-start(bf16[64,1024]{1,0:T(8,128)(2,1)S(1)} %collective-permute-done.4), channel_id=1, source_target_pairs={{0,1},{1,2},{2,3},{3,4},{4,5},{5,6},{6,7},{7,8},{8,9},{9,10},{10,1... | collective-permute-start | bytes 393224 | tf_op jit(solution)/shard_map/ppermute | solution.py:159
  62.5 7.3 %collective-permute-start.12 = (bf16[64,1024]{1,0:T(8,128)(2,1)S(1)}, bf16[64,1024]{1,0:T(8,128)(2,1)S(1)}, u32[]{:S(2)}, u32[]{:S(2)}) collective-permute-start(bf16[64,1024]{1,0:T(8,128)(2,1)S(1)} %collective-permute-done.11), channel_id=1, source_target_pairs={{1,0},{2,1},{3,2},{4,3},{5,4},{6,5},{7,6},{8,7},{9,8},{10,9},{11,1... | collective-permute-start | bytes 393224 | tf_op jit(solution)/shard_map/ppermute | solution.py:161
  69.6 7.2 %collective-permute-start.6 = (bf16[64,1024]{1,0:T(8,128)(2,1)S(1)}, bf16[64,1024]{1,0:T(8,128)(2,1)S(1)}, u32[]{:S(2)}, u32[]{:S(2)}) collective-permute-start(bf16[64,1024]{1,0:T(8,128)(2,1)S(1)} %collective-permute-done.5), channel_id=1, source_target_pairs={{0,1},{1,2},{2,3},{3,4},{4,5},{5,6},{6,7},{7,8},{8,9},{9,10},{10,1... | collective-permute-start | bytes 393224 | tf_op jit(solution)/shard_map/ppermute | solution.py:159
  69.8 7.7 %collective-permute-start.13 = (bf16[64,1024]{1,0:T(8,128)(2,1)S(1)}, bf16[64,1024]{1,0:T(8,128)(2,1)S(1)}, u32[]{:S(2)}, u32[]{:S(2)}) collective-permute-start(bf16[64,1024]{1,0:T(8,128)(2,1)S(1)} %collective-permute-done.12), channel_id=1, source_target_pairs={{1,0},{2,1},{3,2},{4,3},{5,4},{6,5},{7,6},{8,7},{9,8},{10,9},{11,1... | collective-permute-start | bytes 393224 | tf_op jit(solution)/shard_map/ppermute | solution.py:161
  76.8 7.1 %collective-permute-start.7 = (bf16[64,1024]{1,0:T(8,128)(2,1)S(1)}, bf16[64,1024]{1,0:T(8,128)(2,1)S(1)}, u32[]{:S(2)}, u32[]{:S(2)}) collective-permute-start(bf16[64,1024]{1,0:T(8,128)(2,1)S(1)} %collective-permute-done.6), channel_id=1, source_target_pairs={{0,1},{1,2},{2,3},{3,4},{4,5},{5,6},{6,7},{7,8},{8,9},{9,10},{10,1... | collective-permute-start | bytes 393224 | tf_op jit(solution)/shard_map/ppermute | solution.py:159
  77.5 16.4 %collective-permute-start.14 = (bf16[64,1024]{1,0:T(8,128)(2,1)S(1)}, bf16[64,1024]{1,0:T(8,128)(2,1)S(1)}, u32[]{:S(2)}, u32[]{:S(2)}) collective-permute-start(bf16[64,1024]{1,0:T(8,128)(2,1)S(1)} %collective-permute-done.13), channel_id=1, source_target_pairs={{1,0},{2,1},{3,2},{4,3},{5,4},{6,5},{7,6},{8,7},{9,8},{10,9},{11,1... | collective-permute-start | bytes 393224 | tf_op jit(solution)/shard_map/ppermute | solution.py:161
  101.4 0.6 copy-start.16
  110.3 4.2 %copy-start.3 = (bf16[1,512,4,128]{1,3,2,0:T(8,128)(2,1)S(1)}, bf16[1,512,4,128]{1,3,2,0:T(8,128)(2,1)}, u32[]{:S(2)}) copy-start(bf16[1,512,4,128]{1,3,2,0:T(8,128)(2,1)} %copy.285) | copy-start | bytes 1572868 | tf_op jit(solution)/shard_map/while
  114.5 7.2 %copy-start.17 = (s32[4,512]{1,0:T(4,128)S(1)}, s32[4,512]{1,0:T(4,128)}, u32[]{:S(2)}) copy-start(s32[4,512]{1,0:T(4,128)} %copy-done.16) | copy-start | bytes 24580 | tf_op jit(solution)/shard_map/while
  121.7 0.6 copy-start.16
  130.5 4.2 %copy-start.3 = (bf16[1,512,4,128]{1,3,2,0:T(8,128)(2,1)S(1)}, bf16[1,512,4,128]{1,3,2,0:T(8,128)(2,1)}, u32[]{:S(2)}) copy-start(bf16[1,512,4,128]{1,3,2,0:T(8,128)(2,1)} %copy.285) | copy-start | bytes 1572868 | tf_op jit(solution)/shard_map/while
  134.7 8.7 %copy-start.17 = (s32[4,512]{1,0:T(4,128)S(1)}, s32[4,512]{1,0:T(4,128)}, u32[]{:S(2)}) copy-start(s32[4,512]{1,0:T(4,128)} %copy-done.16) | copy-start | bytes 24580 | tf_op jit(solution)/shard_map/while
  143.4 0.6 copy-start.16
  152.3 4.2 %copy-start.3 = (bf16[1,512,4,128]{1,3,2,0:T(8,128)(2,1)S(1)}, bf16[1,512,4,128]{1,3,2,0:T(8,128)(2,1)}, u32[]{:S(2)}) copy-start(bf16[1,512,4,128]{1,3,2,0:T(8,128)(2,1)} %copy.285) | copy-start | bytes 1572868 | tf_op jit(solution)/shard_map/while
  156.5 8.7 %copy-start.17 = (s32[4,512]{1,0:T(4,128)S(1)}, s32[4,512]{1,0:T(4,128)}, u32[]{:S(2)}) copy-start(s32[4,512]{1,0:T(4,128)} %copy-done.16) | copy-start | bytes 24580 | tf_op jit(solution)/shard_map/while
  165.2 0.6 copy-start.16
  174.1 4.2 %copy-start.3 = (bf16[1,512,4,128]{1,3,2,0:T(8,128)(2,1)S(1)}, bf16[1,512,4,128]{1,3,2,0:T(8,128)(2,1)}, u32[]{:S(2)}) copy-start(bf16[1,512,4,128]{1,3,2,0:T(8,128)(2,1)} %copy.285) | copy-start | bytes 1572868 | tf_op jit(solution)/shard_map/while
  178.2 8.7 %copy-start.17 = (s32[4,512]{1,0:T(4,128)S(1)}, s32[4,512]{1,0:T(4,128)}, u32[]{:S(2)}) copy-start(s32[4,512]{1,0:T(4,128)} %copy-done.16) | copy-start | bytes 24580 | tf_op jit(solution)/shard_map/while
  251.0 117.2 %reduce-scatter.6.cloned.1.call-start = ((), (), s32[]{:S(2)}) async-start(), calls=%async_computation.3 | async-start | bytes 2228224 | tf_op jit(solution)/shard_map/reduce_scatter | solution.py:218
  251.2 2.2 copy-start.2
  255.6 0.7 copy-start.19
  255.6 0.9 copy-start.7
  255.6 1.3 copy-start.18
  255.6 1.5 copy-start.28
  255.6 1.6 copy-start.5
  255.6 1.5 copy-start.24
  255.6 127.9 %reduce-scatter.8.cloned.1.call-start = ((), (), s32[]{:S(2)}) async-start(), calls=%async_computation.4 | async-start | bytes 393216 | tf_op jit(solution)/shard_map/reduce_scatter | solution.py:241
  256.5 3.1 copy-start.22
  256.9 2.9 copy-start.14
  257.2 3.0 copy-start.27
  257.2 3.0 copy-start.30
  257.2 3.3 copy-start.9
  257.2 3.3 copy-start.11
  257.2 3.3 copy-start.21
  260.1 1.8 copy-start.36
  368.7 16.5 %copy-start.1 = (bf16[2048,512]{1,0:T(8,128)(2,1)S(1)}, bf16[2048,512]{1,0:T(8,128)(2,1)}, u32[]{:S(2)}) copy-start(bf16[2048,512]{1,0:T(8,128)(2,1)} %param.21) | copy-start | bytes 6291460
  368.7 4.1 %copy-start.25 = (f32[2,32]{1,0:T(2,128)S(1)}, f32[2,32]{1,0:T(2,128)}, u32[]{:S(2)}) copy-start(f32[2,32]{1,0:T(2,128)} %get-tuple-element.185) | copy-start | bytes 772
  368.7 14.9 %copy-start.12 = (bf16[64,1024]{1,0:T(8,128)(2,1)S(1)}, bf16[64,1024]{1,0:T(8,128)(2,1)}, u32[]{:S(2)}) copy-start(bf16[64,1024]{1,0:T(8,128)(2,1)} %param.18) | copy-start | bytes 393220
Sparse Core Ops, SparseCore 0:
  251.1 52.6 reduce-scatter.9
  307.5 60.6 reduce-scatter.5
  372.9 10.6 reduce-scatter.7
